TPU v7x, 128 devices: a whole 4x4x4 slice. The times are simulated.
128 devices in a mesh: occ: 4 (over x), vir: 32 (over y, z, core).
Axes of the slice: x: 4, y: 4, z: 4, core: 2. Of those that a mesh axis runs over, the one named last changes fastest.
Arguments:
- amplitudes: bfloat16 [256, 262144], P('occ', 'vir'), may hold values from -6 to 6
- cycle_integrals: bfloat16 [16, 64, 16, 64], P(None, None, 'occ'), may hold values from -0.1875 to 0.1875
- ladder_tiles: bfloat16 [2048, 4, 128, 128], P('vir'), may hold values from -0.25 to 0.25
- ladder_rows: int32 [2048, 4], P('vir'), may hold values from 0 to 2047, as said below
- ladder_count: int32 [2048], P('vir'), may hold values from 2 to 4
- row_gap: float32 [256], P('occ'), may hold values from 1 to 3
- column_energy: float32 [262144], P('vir'), may hold values from 0.5 to 8
Outputs:
- updated: bfloat16 [256, 262144], P('occ', 'vir')
Inputs may be any that keep to these rules, and one draw needn't show every extreme that they name: `ladder_rows`: each entry of column tile c's list names a virtual-pair tile within 2 tiles of c; entry 0 is max(c - 2, 0) and entry 1 is min(c + 2, 2047).
All inputs are finite; a program needn't handle non-finite values.
Results may differ from a plain program's by a relative error of at most 0.0019.
Values may be sent and summed in bfloat16 or wider, within the bound.
A program may use at most 192 MiB of HBM per device.

v0:
```python
import jax
import jax.numpy as jnp
from jax import lax
from jax.sharding import PartitionSpec as P

TILE = 128
NJ = 16
NA = 4096
NB_DEV = 2
KMAX = 4
HT = 2


def extended(block, sides, width):
    for axis, dim in sides:
        count = lax.axis_size(axis)
        forward = [(i, i + 1) for i in range(count - 1)]
        backward = [(target, source) for source, target in forward]
        low = lax.ppermute(
            lax.slice_in_dim(block, block.shape[dim] - width, None, axis=dim), axis, forward
        )
        high = lax.ppermute(lax.slice_in_dim(block, 0, width, axis=dim), axis, backward)
        block = jnp.concatenate([low, block, high], axis=dim)
    return block


def local(
    amplitudes, cycle_integrals, ladder_tiles, ladder_rows, ladder_count, row_gap, column_energy
):
    rows_dev = amplitudes.shape[0]
    cols_dev = amplitudes.shape[1]
    outer_occ = rows_dev // NJ
    four_dim = amplitudes.reshape(outer_occ, NJ, NB_DEV, NA)
    cycle_input = lax.all_to_all(four_dim, "vir", split_axis=3, concat_axis=2, tiled=True)
    tiles_dev = cols_dev // TILE
    padded = extended(amplitudes, (("vir", 1),), HT * TILE)
    own_tiles = lax.axis_index("vir") * tiles_dev + jnp.arange(tiles_dev, dtype=jnp.int32)
    relative = ladder_rows - own_tiles[:, None]
    live_mask = jnp.arange(KMAX, dtype=jnp.int32)[None, :] < ladder_count[:, None]
    ladder = jnp.zeros((rows_dev, tiles_dev, TILE), jnp.float32)
    for offset in range(2 * HT + 1):
        window = padded[:, offset * TILE : offset * TILE + cols_dev].reshape(
            rows_dev, tiles_dev, TILE
        )
        for entry in range(KMAX):
            selected = live_mask[:, entry] & (relative[:, entry] == offset - HT)
            masked = jnp.where(
                selected[:, None, None], ladder_tiles[:, entry], jnp.zeros((), jnp.bfloat16)
            )
            ladder = ladder + jnp.einsum(
                "rcp,cpq->rcq", window, masked, preferred_element_type=jnp.float32
            )
    ladder = ladder.reshape(rows_dev, cols_dev)
    all_rows = lax.all_gather(cycle_input, "occ", axis=0, tiled=True)
    cycle_part = jnp.einsum(
        "ijba,jbkc->ikca", all_rows, cycle_integrals, preferred_element_type=jnp.float32
    ).astype(jnp.bfloat16)
    cycle_pair = lax.all_to_all(
        lax.all_to_all(cycle_part, "occ", split_axis=0, concat_axis=1, tiled=True),
        "vir",
        split_axis=2,
        concat_axis=3,
        tiled=True,
    )
    cycle_flat = cycle_pair.reshape(rows_dev, cols_dev)
    denominator = row_gap[:, None] + column_energy[None, :]
    updated = (
        amplitudes.astype(jnp.float32) + (cycle_flat.astype(jnp.float32) + ladder) / denominator
    )
    return updated.astype(jnp.bfloat16)


def solution(mesh):
    in_specs = (
        P("occ", "vir"),
        P(None, None, "occ", None),
        P("vir", None, None, None),
        P("vir", None),
        P("vir"),
        P("occ"),
        P("vir"),
    )
    out_specs = P("occ", "vir")
    return jax.shard_map(local, mesh=mesh, in_specs=in_specs, out_specs=out_specs, check_vma=False)
```

profile of v0, /device:TPU:1, one launch (start us, length us, event | category | flops | bytes accessed | tf_op | source)
XLA Modules:
  0.0 195.1 jit_solution(11123908715003614297)
XLA Ops:
  6.5 0.8 fusion.152
  7.3 4.9 %collective-permute-start = (bf16[64,256]{1,0:T(8,128)(2,1)S(1)}, bf16[64,256]{1,0:T(8,128)(2,1)S(1)}, u32[]{:S(2)}, u32[]{:S(2)}) collective-permute-start(bf16[64,256]{1,0:T(8,128)(2,1)S(1)} %get-tuple-element.11), channel_id=1, source_target_pairs={{0,1},{1,2},{2,3},{3,4},{4,5},{5,6},{6,7},{7,8},{8,9},{9,10},{10,1... | collective-permute-start | bytes 98312 | tf_op jit(solution)/shard_map/ppermute | solution.py:19
  12.2 1.9 collective-permute-start.1
  14.2 1.8 reshape.294
  16.0 9.4 %copy.133 = bf16[4,16,2,4096]{1,0,2,3:T(4,128)(2,1)} copy(bf16[4,16,2,4096]{3,2,1,0:T(2,128)(2,1)S(1)} %reshape.294) | data formatting | bytes 2097152 | tf_op jit(solution)/shard_map/reshape | solution.py:33
  25.5 11.2 %reshape.306 = bf16[32,2,8192]{2,1,0:T(2,128)(2,1)} reshape(bf16[4096,2,4,16]{3,2,1,0:T(4,128)(2,1)} %bitcast.213) | data formatting | bytes 2097152
  36.7 8.4 %all-to-all-start = ((bf16[32,2,8192]{2,1,0:T(2,128)(2,1)}), bf16[32,2,8192]{2,1,0:T(2,128)(2,1)S(1)}, u32[]{:S(2)}, u32[]{:S(2)}) async-start(bf16[32,2,8192]{2,1,0:T(2,128)(2,1)} %reshape.306), calls=%async_computation | async-start | bytes 2097152 | tf_op jit(solution)/shard_map/all_to_all | solution.py:34
  45.1 0.0 all-gather.2.cloned.1.call-start
  45.2 0.0 copy-done.7
  45.2 0.0 copy-done.4
  45.3 0.0 copy-done
  45.3 3.7 %fusion.12 = f32[64,128,64]{1,2,0:T(8,128)} fusion(pred[64]{0:T(512)(128)(4,1)S(1)} %get-tuple-element.23, bf16[64,4,128,128]{3,2,1,0:T(8,128)(2,1)} %param.9, bf16[64,8192]{1,0:T(8,128)(2,1)S(1)} %copy-done), kind=kOutput, calls=%fused_computation.23 | convolution fusion | flops 135266304 | bytes 5242944 | tf_op jit(solution)/shard_map/rcp,cpq->rcq/dot_general | solution.py:50
  49.0 3.6 %fusion.17 = f32[64,128,64]{1,2,0:T(8,128)} fusion(pred[64]{0:T(512)(128)(4,1)S(1)} %get-tuple-element.15, bf16[64,4,128,128]{3,2,1,0:T(8,128)(2,1)} %param.9, bf16[64,8192]{1,0:T(8,128)(2,1)S(1)} %copy-done), kind=kOutput, calls=%fused_computation.33 | convolution fusion | flops 135266304 | bytes 5242944 | tf_op jit(solution)/shard_map/rcp,cpq->rcq/dot_general | solution.py:50
  52.7 3.7 %fusion.23 = f32[64,128,64]{1,2,0:T(8,128)} fusion(pred[64]{0:T(512)(128)(4,1)S(1)} %get-tuple-element.19, bf16[64,4,128,128]{3,2,1,0:T(8,128)(2,1)} %param.9, bf16[64,8192]{1,0:T(8,128)(2,1)S(1)} %copy-done), kind=kOutput, calls=%fused_computation.48 | convolution fusion | flops 135266304 | bytes 5242944 | tf_op jit(solution)/shard_map/rcp,cpq->rcq/dot_general | solution.py:50
  56.3 5.7 %all-to-all-done = bf16[32,2,8192]{2,1,0:T(2,128)(2,1)S(1)} async-done(((bf16[32,2,8192]{2,1,0:T(2,128)(2,1)}), bf16[32,2,8192]{2,1,0:T(2,128)(2,1)S(1)}, u32[]{:S(2)}, u32[]{:S(2)}) %all-to-all-start) | async-done | bytes 1048608 | tf_op jit(solution)/shard_map/all_to_all | solution.py:34
  62.0 7.6 %reshape.307 = bf16[4096,2,4,16]{3,2,1,0:T(4,128)(2,1)} reshape(bf16[32,2,8192]{2,1,0:T(2,128)(2,1)S(1)} %all-to-all-done) | data formatting | bytes 2097152
  69.6 12.8 %copy.134 = bf16[4,16,32,2,128]{4,3,2,1,0:T(2,128)(2,1)} copy(bf16[4,16,32,2,128]{1,0,3,4,2:T(4,128)(2,1)} %bitcast.214) | data formatting | bytes 2097152 | tf_op jit(solution)/shard_map/all_to_all | solution.py:34
  82.4 0.0 all-gather.2.cloned.1.call-update
  82.4 0.0 slice-start
  82.4 3.9 %fusion.7 = f32[64,128,64]{1,2,0:T(8,128)} fusion(pred[64]{0:T(512)(128)(4,1)S(1)} %get-tuple-element.27, bf16[64,4,128,128]{3,2,1,0:T(8,128)(2,1)} %param.9, bf16[64,8192]{1,0:T(8,128)(2,1)S(1)} %copy-done), kind=kOutput, calls=%fused_computation.13 | convolution fusion | flops 135266304 | bytes 5242944 | tf_op jit(solution)/shard_map/rcp,cpq->rcq/dot_general | solution.py:50
  86.3 0.0 collective-permute-done
  86.3 0.0 slice-start.1
  86.4 0.1 constant_dynamic-update-slice_fusion
  86.5 0.0 collective-permute-done.1
  86.5 0.4 slice_bitcast_fusion.1
  86.9 0.0 copy-start.1
  86.9 0.3 slice_bitcast_fusion.3
  87.2 0.0 copy-start.2
  87.2 0.0 slice-done
  87.2 2.2 %slice-done.1 = s8[4194304]{0:T(1024)(128)(4,1)S(1)} async-done(((s8[8388608]{0:T(1024)(128)(4,1)}), s8[4194304]{0:T(1024)(128)(4,1)S(1)}, s32[]{:S(2)}) %slice-start.1) | async-done | bytes 4194328
  89.4 2.1 %fusion.13 = f32[64,128,64]{1,2,0:T(8,128)} fusion(pred[64]{0:T(512)(128)(4,1)S(1)} %get-tuple-element.24, bf16[64,4,128,128]{3,2,1,0:T(8,128)(2,1)S(1)} %bitcast.220, bf16[8,64,8,128]{3,2,1,0:T(8,128)(2,1)S(1)} %get-tuple-element.7), kind=kOutput, calls=%fused_computation.24 | convolution fusion | flops 135266304 | bytes 5243392 | tf_op jit(solution)/shard_map/rcp,cpq->rcq/dot_general | solution.py:50
  91.5 2.1 %fusion.18 = f32[64,128,64]{1,2,0:T(8,128)} fusion(pred[64]{0:T(512)(128)(4,1)S(1)} %get-tuple-element.16, bf16[64,4,128,128]{3,2,1,0:T(8,128)(2,1)S(1)} %bitcast.220, bf16[8,64,8,128]{3,2,1,0:T(8,128)(2,1)S(1)} %get-tuple-element.7), kind=kOutput, calls=%fused_computation.34 | convolution fusion | flops 135266304 | bytes 5243392 | tf_op jit(solution)/shard_map/rcp,cpq->rcq/dot_general | solution.py:50
  93.6 2.1 %fusion.14 = f32[64,128,64]{1,2,0:T(8,128)} fusion(pred[64]{0:T(512)(128)(4,1)S(1)} %get-tuple-element.25, bf16[64,4,128,128]{3,2,1,0:T(8,128)(2,1)S(1)} %bitcast.220, bf16[8,64,8,128]{3,2,1,0:T(8,128)(2,1)S(1)} %get-tuple-element.8), kind=kOutput, calls=%fused_computation.25 | convolution fusion | flops 135266304 | bytes 5243392 | tf_op jit(solution)/shard_map/rcp,cpq->rcq/dot_general | solution.py:50
  95.7 2.1 %fusion.19 = f32[64,128,64]{1,2,0:T(8,128)} fusion(pred[64]{0:T(512)(128)(4,1)S(1)} %get-tuple-element.17, bf16[64,4,128,128]{3,2,1,0:T(8,128)(2,1)S(1)} %bitcast.220, bf16[8,64,8,128]{3,2,1,0:T(8,128)(2,1)S(1)} %get-tuple-element.8), kind=kOutput, calls=%fused_computation.35 | convolution fusion | flops 135266304 | bytes 5243392 | tf_op jit(solution)/shard_map/rcp,cpq->rcq/dot_general | solution.py:50
  97.8 2.1 %fusion.24 = f32[64,128,64]{1,2,0:T(8,128)} fusion(pred[64]{0:T(512)(128)(4,1)S(1)} %get-tuple-element.20, bf16[64,4,128,128]{3,2,1,0:T(8,128)(2,1)S(1)} %bitcast.220, bf16[8,64,8,128]{3,2,1,0:T(8,128)(2,1)S(1)} %get-tuple-element.7), kind=kOutput, calls=%fused_computation.49 | convolution fusion | flops 135266304 | bytes 5243392 | tf_op jit(solution)/shard_map/rcp,cpq->rcq/dot_general | solution.py:50
  99.9 2.1 %fusion.8 = f32[64,128,64]{1,2,0:T(8,128)} fusion(pred[64]{0:T(512)(128)(4,1)S(1)} %get-tuple-element.28, bf16[64,4,128,128]{3,2,1,0:T(8,128)(2,1)S(1)} %bitcast.220, bf16[8,64,8,128]{3,2,1,0:T(8,128)(2,1)S(1)} %get-tuple-element.7), kind=kOutput, calls=%fused_computation.14 | convolution fusion | flops 135266304 | bytes 5243392 | tf_op jit(solution)/shard_map/rcp,cpq->rcq/dot_general | solution.py:50
  102.0 0.0 copy-done.1
  102.0 2.1 %fusion.9 = f32[64,128,64]{1,2,0:T(8,128)} fusion(pred[64]{0:T(512)(128)(4,1)S(1)} %get-tuple-element.29, bf16[64,4,128,128]{3,2,1,0:T(8,128)(2,1)S(1)} %bitcast.220, bf16[8,64,8,128]{3,2,1,0:T(8,128)(2,1)S(1)} %get-tuple-element.8), kind=kOutput, calls=%fused_computation.15 | convolution fusion | flops 135266304 | bytes 5243392 | tf_op jit(solution)/shard_map/rcp,cpq->rcq/dot_general | solution.py:50
  104.1 2.1 %fusion.11 = f32[64,128,64]{1,2,0:T(8,128)} fusion(pred[64]{0:T(512)(128)(4,1)S(1)} %get-tuple-element.21, bf16[64,4,128,128]{3,2,1,0:T(8,128)(2,1)S(1)} %bitcast.220, bf16[8,64,8,128]{3,2,1,0:T(8,128)(2,1)S(1)} %get-tuple-element.6), kind=kOutput, calls=%fused_computation.22 | convolution fusion | flops 135266304 | bytes 5243392 | tf_op jit(solution)/shard_map/rcp,cpq->rcq/dot_general | solution.py:50
  106.2 2.1 %fusion.16 = f32[64,128,64]{1,2,0:T(8,128)} fusion(pred[64]{0:T(512)(128)(4,1)S(1)} %get-tuple-element.14, bf16[64,4,128,128]{3,2,1,0:T(8,128)(2,1)S(1)} %bitcast.220, bf16[8,64,8,128]{3,2,1,0:T(8,128)(2,1)S(1)} %get-tuple-element.6), kind=kOutput, calls=%fused_computation.32 | convolution fusion | flops 135266304 | bytes 5243392 | tf_op jit(solution)/shard_map/rcp,cpq->rcq/dot_general | solution.py:50
  108.3 0.0 copy-done.2
  108.3 2.0 %fusion.22 = f32[64,128,64]{1,2,0:T(8,128)} fusion(pred[64]{0:T(512)(128)(4,1)S(1)} %get-tuple-element.18, bf16[64,4,128,128]{3,2,1,0:T(8,128)(2,1)S(1)} %bitcast.220, bf16[8,64,8,128]{3,2,1,0:T(8,128)(2,1)S(1)} %get-tuple-element.6), kind=kOutput, calls=%fused_computation.47 | convolution fusion | flops 135266304 | bytes 5243392 | tf_op jit(solution)/shard_map/rcp,cpq->rcq/dot_general | solution.py:50
  110.4 2.1 %fusion.21 = f32[64,128,64]{1,2,0:T(8,128)} fusion(pred[64]{0:T(512)(128)(4,1)S(1)} %get-tuple-element.22, bf16[64,4,128,128]{3,2,1,0:T(8,128)(2,1)S(1)} %bitcast.220, bf16[8,64,8,128]{3,2,1,0:T(8,128)(2,1)S(1)} %get-tuple-element.5), kind=kOutput, calls=%fused_computation.46 | convolution fusion | flops 135266304 | bytes 5243392 | tf_op jit(solution)/shard_map/rcp,cpq->rcq/dot_general | solution.py:50
  112.5 2.0 %fusion.5 = f32[64,128,64]{1,2,0:T(8,128)} fusion(pred[64]{0:T(512)(128)(4,1)S(1)} %get-tuple-element.30, bf16[64,4,128,128]{3,2,1,0:T(8,128)(2,1)S(1)} %bitcast.220, bf16[8,64,8,128]{3,2,1,0:T(8,128)(2,1)S(1)} %get-tuple-element.5), kind=kOutput, calls=%fused_computation.11 | convolution fusion | flops 135266304 | bytes 5243392 | tf_op jit(solution)/shard_map/rcp,cpq->rcq/dot_general | solution.py:50
  114.5 13.9 %all-gather.2.cloned.1.call-done = bf16[16,16,64,128]{3,2,1,0:T(8,128)(2,1)} async-done(((bf16[4,16,64,128]{3,2,1,0:T(8,128)(2,1)}), bf16[16,16,64,128]{3,2,1,0:T(8,128)(2,1)}) %all-gather.2.cloned.1.call-update) | async-done | bytes 4194320 | tf_op jit(solution)/shard_map/all_gather | solution.py:54
  128.4 0.0 copy-done.6
  128.4 3.5 %fusion.48 = bf16[16,4,64,128]{3,2,0,1:T(8,128)(2,1)S(1)} fusion(bf16[16,16,64,128]{3,2,1,0:T(8,128)(2,1)} %all-gather.2.cloned.1.call-done, bf16[16,64,4,64,1]{3,2,1,0,4:T(4,128)(2,1)S(1)} %bitcast.221), kind=kOutput, calls=%fused_computation.72 | convolution fusion | flops 1074266112 | bytes 5767168 | tf_op jit(solution)/shard_map/ijba,jbkc->ikca/dot_general | solution.py:55
  131.8 1.0 copy.136
  132.9 3.7 %all-to-all-start.1 = ((bf16[16,4,64,128]{3,2,1,0:T(8,128)(2,1)}), bf16[16,4,64,128]{3,2,1,0:T(8,128)(2,1)S(1)}, u32[]{:S(2)}, u32[]{:S(2)}) async-start(bf16[16,4,64,128]{3,2,1,0:T(8,128)(2,1)} %copy.136), calls=%async_computation.1 | async-start | bytes 2097152 | tf_op jit(solution)/shard_map/all_to_all | solution.py:59
  136.6 4.0 %fusion.6 = f32[64,128,64]{1,2,0:T(8,128)} fusion(pred[64]{0:T(512)(128)(4,1)S(1)} %get-tuple-element.26, bf16[64,4,128,128]{3,2,1,0:T(8,128)(2,1)} %param.9, bf16[8,64,8,128]{3,2,1,0:T(8,128)(2,1)} %copy-done.2), kind=kOutput, calls=%fused_computation.12 | convolution fusion | flops 135266304 | bytes 5242944 | tf_op jit(solution)/shard_map/rcp,cpq->rcq/dot_general | solution.py:50
  140.7 3.6 %fusion.10 = f32[64,128,64]{1,2,0:T(8,128)} fusion(pred[64]{0:T(512)(128)(4,1)S(1)} %get-tuple-element.32, bf16[64,4,128,128]{3,2,1,0:T(8,128)(2,1)} %param.9, bf16[8,64,8,128]{3,2,1,0:T(8,128)(2,1)S(1)} %get-tuple-element.5), kind=kOutput, calls=%fused_computation.21 | convolution fusion | flops 135266304 | bytes 5242944 | tf_op jit(solution)/shard_map/rcp,cpq->rcq/dot_general | solution.py:50
  144.3 3.6 %fusion.15 = f32[64,128,64]{1,2,0:T(8,128)} fusion(pred[64]{0:T(512)(128)(4,1)S(1)} %get-tuple-element.31, bf16[64,4,128,128]{3,2,1,0:T(8,128)(2,1)} %param.9, bf16[8,64,8,128]{3,2,1,0:T(8,128)(2,1)S(1)} %get-tuple-element.5), kind=kOutput, calls=%fused_computation.31 | convolution fusion | flops 135266304 | bytes 5242944 | tf_op jit(solution)/shard_map/rcp,cpq->rcq/dot_general | solution.py:50
  147.9 2.9 %all-to-all-done.1 = bf16[16,4,64,128]{3,2,1,0:T(8,128)(2,1)S(1)} async-done(((bf16[16,4,64,128]{3,2,1,0:T(8,128)(2,1)}), bf16[16,4,64,128]{3,2,1,0:T(8,128)(2,1)S(1)}, u32[]{:S(2)}, u32[]{:S(2)}) %all-to-all-start.1) | async-done | bytes 1048608 | tf_op jit(solution)/shard_map/all_to_all | solution.py:59
  150.9 0.1 copy.137
  151.0 1.6 copy.138
  152.6 8.6 %all-to-all-start.2 = ((bf16[4,16,64,128]{3,1,0,2:T(8,128)(2,1)}), bf16[4,16,64,128]{3,1,0,2:T(8,128)(2,1)}, u32[]{:S(2)}, u32[]{:S(2)}) async-start(bf16[4,16,64,128]{3,1,0,2:T(8,128)(2,1)} %copy.138), calls=%async_computation.2 | async-start | bytes 2097152 | tf_op jit(solution)/shard_map/all_to_all | solution.py:58
  161.3 15.6 %fusion.20 = f32[64,8,8,128]{3,2,1,0:T(8,128)S(1)} fusion(f32[64,128,64]{1,2,0:T(8,128)} %fusion.9, f32[64,128,64]{1,2,0:T(8,128)} %fusion.14, f32[64,128,64]{1,2,0:T(8,128)} %fusion.19, f32[64,128,64]{1,2,0:T(8,128)} %fusion.8, f32[64,128,64]{1,2,0:T(8,128)} %fusion.13, f32[64,128,64]{1,2,0:T(8,128)} %fusion.24, f32[64,128,64]{1,2,0:T(8,128)} %fusion.18, ...), kind=kOutput, calls=%fused_computation.38 | convolution fusion | flops 145227776 | bytes 45088832 | tf_op jit(solution)/shard_map/rcp,cpq->rcq/dot_general | solution.py:50
  176.9 1.4 all-to-all-done.2
  178.2 1.4 copy.139
  179.6 0.3 convert_bitcast_fusion
  179.9 2.6 %copy.140 = f32[4,16,2,32,128]{4,3,2,1,0:T(8,128)} copy(f32[4,16,2,32,128]{4,1,2,3,0:T(8,128)S(1)} %convert_bitcast_fusion) | data formatting | bytes 4194304 | tf_op jit(solution)/shard_map/convert_element_type | solution.py:68
  182.5 2.7 %reshape.301 = f32[64,8192]{1,0:T(8,128)} reshape(f32[4,16,2,32,128]{4,3,2,1,0:T(8,128)} %copy.140) | data formatting | bytes 4194304 | tf_op jit(solution)/shard_map/convert_element_type | solution.py:68
  185.2 0.0 copy-done.5
  185.2 3.1 %fusion.4 = bf16[64,8192]{1,0:T(8,128)(2,1)} fusion(f32[64,8192]{1,0:T(8,128)} %reshape.301, f32[64,8,8,128]{3,2,1,0:T(8,128)S(1)} %fusion.20, bf16[64,8192]{1,0:T(8,128)(2,1)S(1)} %copy-done, f32[8192]{0:T(1024)S(1)} %copy-done.3, f32[64]{0:T(128)S(1)} %copy-done.5), kind=kLoop, calls=%fused_computation.5 | loop fusion | flops 3145728 | bytes 6324480 | tf_op jit(solution)/shard_map/convert_element_type | solution.py:70
  (16 shorter events, 0.1 us)
Async XLA Ops:
  7.3 79.0 %collective-permute-start = (bf16[64,256]{1,0:T(8,128)(2,1)S(1)}, bf16[64,256]{1,0:T(8,128)(2,1)S(1)}, u32[]{:S(2)}, u32[]{:S(2)}) collective-permute-start(bf16[64,256]{1,0:T(8,128)(2,1)S(1)} %get-tuple-element.11), channel_id=1, source_target_pairs={{0,1},{1,2},{2,3},{3,4},{4,5},{5,6},{6,7},{7,8},{8,9},{9,10},{10,1... | collective-permute-start | bytes 98312 | tf_op jit(solution)/shard_map/ppermute | solution.py:19
  12.2 74.3 %collective-permute-start.1 = (bf16[64,256]{1,0:T(8,128)(2,1)S(1)}, bf16[64,256]{1,0:T(8,128)(2,1)S(1)}, u32[]{:S(2)}, u32[]{:S(2)}) collective-permute-start(bf16[64,256]{1,0:T(8,128)(2,1)S(1)} %get-tuple-element.12), channel_id=1, source_target_pairs={{1,0},{2,1},{3,2},{4,3},{5,4},{6,5},{7,6},{8,7},{9,8},{10,9},{11,1... | collective-permute-start | bytes 98312 | tf_op jit(solution)/shard_map/ppermute | solution.py:22
  36.7 8.5 %copy-start.7 = (s32[64]{0:T(128)S(1)}, s32[64]{0:T(128)}, u32[]{:S(2)}) copy-start(s32[64]{0:T(128)} %param.11) | copy-start | bytes 772
  36.7 8.5 %copy-start.4 = (s32[64,4]{0,1:T(4,128)S(1)}, s32[64,4]{0,1:T(4,128)}, u32[]{:S(2)}) copy-start(s32[64,4]{0,1:T(4,128)} %param.10) | copy-start | bytes 3076
  36.7 8.6 %copy-start = (bf16[64,8192]{1,0:T(8,128)(2,1)S(1)}, bf16[64,8192]{1,0:T(8,128)(2,1)}, u32[]{:S(2)}) copy-start(bf16[64,8192]{1,0:T(8,128)(2,1)} %param.7) | copy-start | bytes 3145732
  36.7 25.4 %all-to-all-start = ((bf16[32,2,8192]{2,1,0:T(2,128)(2,1)}), bf16[32,2,8192]{2,1,0:T(2,128)(2,1)S(1)}, u32[]{:S(2)}, u32[]{:S(2)}) async-start(bf16[32,2,8192]{2,1,0:T(2,128)(2,1)} %reshape.306), calls=%async_computation | async-start | bytes 2097152 | tf_op jit(solution)/shard_map/all_to_all | solution.py:34
  45.1 83.3 %all-gather.2.cloned.1.call-start = ((), (), s32[]{:S(2)}) async-start(), calls=%async_computation.3 | async-start | bytes 5242880 | tf_op jit(solution)/shard_map/all_gather | solution.py:54
  82.4 4.8 %slice-start = ((s8[8388608]{0:T(1024)(128)(4,1)}), s8[4194304]{0:T(1024)(128)(4,1)S(1)}, s32[]{:S(2)}) async-start(s8[8388608]{0:T(1024)(128)(4,1)} %bitcast.219), calls=%async_computation.4 | async-start | bytes 8388608
  86.3 3.1 %slice-start.1 = ((s8[8388608]{0:T(1024)(128)(4,1)}), s8[4194304]{0:T(1024)(128)(4,1)S(1)}, s32[]{:S(2)}) async-start(s8[8388608]{0:T(1024)(128)(4,1)} %bitcast.219), calls=%async_computation.5 | async-start | bytes 8388608
  86.9 15.1 %copy-start.1 = (bf16[8,64,8,128]{3,2,1,0:T(8,128)(2,1)}, bf16[8,64,8,128]{3,2,1,0:T(8,128)(2,1)S(1)}, u32[]{:S(2)}) copy-start(bf16[8,64,8,128]{3,2,1,0:T(8,128)(2,1)S(1)} %get-tuple-element.8) | copy-start | bytes 3145732
  87.2 21.1 %copy-start.2 = (bf16[8,64,8,128]{3,2,1,0:T(8,128)(2,1)}, bf16[8,64,8,128]{3,2,1,0:T(8,128)(2,1)S(1)}, u32[]{:S(2)}) copy-start(bf16[8,64,8,128]{3,2,1,0:T(8,128)(2,1)S(1)} %get-tuple-element.6) | copy-start | bytes 3145732
  112.5 15.9 %copy-start.6 = (bf16[16,64,4,64]{3,2,1,0:T(4,128)(2,1)S(1)}, bf16[16,64,4,64]{3,2,1,0:T(4,128)(2,1)}, u32[]{:S(2)}) copy-start(bf16[16,64,4,64]{3,2,1,0:T(4,128)(2,1)} %param.8) | copy-start | bytes 1572868
  132.9 18.0 %all-to-all-start.1 = ((bf16[16,4,64,128]{3,2,1,0:T(8,128)(2,1)}), bf16[16,4,64,128]{3,2,1,0:T(8,128)(2,1)S(1)}, u32[]{:S(2)}, u32[]{:S(2)}) async-start(bf16[16,4,64,128]{3,2,1,0:T(8,128)(2,1)} %copy.136), calls=%async_computation.1 | async-start | bytes 2097152 | tf_op jit(solution)/shard_map/all_to_all | solution.py:59
  152.6 25.6 %all-to-all-start.2 = ((bf16[4,16,64,128]{3,1,0,2:T(8,128)(2,1)}), bf16[4,16,64,128]{3,1,0,2:T(8,128)(2,1)}, u32[]{:S(2)}, u32[]{:S(2)}) async-start(bf16[4,16,64,128]{3,1,0,2:T(8,128)(2,1)} %copy.138), calls=%async_computation.2 | async-start | bytes 2097152 | tf_op jit(solution)/shard_map/all_to_all | solution.py:58
  182.5 2.7 %copy-start.3 = (f32[8192]{0:T(1024)S(1)}, f32[8192]{0:T(1024)}, u32[]{:S(2)}) copy-start(f32[8192]{0:T(1024)} %param.13) | copy-start | bytes 98308
  182.5 2.7 %copy-start.5 = (f32[64]{0:T(128)S(1)}, f32[64]{0:T(128)}, u32[]{:S(2)}) copy-start(f32[64]{0:T(128)} %param.12) | copy-start | bytes 772
Sparse Core Ops, SparseCore 0:
  82.6 45.7 all-gather.1
where the time goes:
time: 196 us; the launch traced here: 195 us
  matrix products  70.3 us (36%)
  local copies, waits for them, and re-layouts  56.1 us (29%)
  starting transfers between devices  27.7 us (14%)
  waiting for transfers between devices  23.9 us (12%)
  between operations  13.7 us (7%)
  other arithmetic  3.39 us (2%)
    dot_general x20, matrix products, local(): jnp.einsum('rcp,cpq->rcq', window, masked, preferred_element_type=jnp.flo...  66.9 us
    unnamed x25, local copies, waits for them, and re-layouts  21.7 us
    all_gather x1, waiting for transfers between devices, local(): all_rows = lax.all_gather(cycle_input, 'occ', axis=0, tiled=True)  13.9 us
    all_to_all x1, local copies, waits for them, and re-layouts, local(): lax.all_to_all(four_dim, 'vir', split_axis=3, concat_axis=2, tiled=True)  12.8 us
    reshape x2, local copies, waits for them, and re-layouts, local(): four_dim = amplitudes.reshape(outer_occ, NJ, NB_DEV, NA)  11.3 us
    all_to_all x1, starting transfers between devices, local(): lax.all_to_all(lax.all_to_all(cycle_part, 'occ', split_axis=0, concat_axi...  8.64 us
    all_to_all x1, starting transfers between devices, local(): lax.all_to_all(four_dim, 'vir', split_axis=3, concat_axis=2, tiled=True)  8.45 us
    all_to_all x1, waiting for transfers between devices, local(): lax.all_to_all(four_dim, 'vir', split_axis=3, concat_axis=2, tiled=True)  5.69 us
  transfers between devices with their start and end apart: 6, of which 4 were waited for; matrix products, arithmetic and copies ran while one was open for 57% of the time, Pallas kernels for 0%

commit v1 on v0

--- a/solution.py
+++ b/solution.py
@@ -9,6 +9,11 @@
 NB_DEV = 2
 KMAX = 4
 HT = 2
+
+
+def tiled_gather(x, axis, dim):
+    copies = jnp.concatenate([x] * lax.axis_size(axis), axis=dim)
+    return lax.all_to_all(copies, axis, dim, dim, tiled=True)
 
 
 def extended(block, sides, width):
@@ -51,7 +56,7 @@
                 "rcp,cpq->rcq", window, masked, preferred_element_type=jnp.float32
             )
     ladder = ladder.reshape(rows_dev, cols_dev)
-    all_rows = lax.all_gather(cycle_input, "occ", axis=0, tiled=True)
+    all_rows = tiled_gather(cycle_input, "occ", 0)
     cycle_part = jnp.einsum(
         "ijba,jbkc->ikca", all_rows, cycle_integrals, preferred_element_type=jnp.float32
     ).astype(jnp.bfloat16)

time: 196 us -> 205 us (1.046)
  between operations: 13.7 us -> 0.27 us
  matrix products: 70.3 us -> 80.7 us
  waiting for transfers between devices: 23.9 us -> 29.5 us
  starting transfers between devices: 27.7 us -> 32.8 us
  other arithmetic: 3.39 us -> 5.67 us
    all_to_all x0 -> x1, waiting for transfers between devices: none -> 25.5 us  [tiled_gather(): return lax.all_to_all(copies, axis, dim, dim, tiled=True)]
    all_gather x1 -> x0, waiting for transfers between devices: 13.9 us -> none  [local(): all_rows = lax.all_gather(cycle_input, 'occ', axis=0, tiled=True)]
    dot_general x20, matrix products: 66.9 us -> 76.3 us  [local(): jnp.einsum('rcp,cpq->rcq', window, masked, preferred_element_type=jnp.flo...]
    all_to_all x1, waiting for transfers between devices: 5.69 us -> 0.01 us  [local(): lax.all_to_all(four_dim, 'vir', split_axis=3, concat_axis=2, tiled=True)]
    all_to_all x0 -> x1, starting transfers between devices: none -> 5.03 us  [tiled_gather(): return lax.all_to_all(copies, axis, dim, dim, tiled=True)]
    concatenate x0 -> x1, other arithmetic: none -> 2.28 us  [tiled_gather(): copies = jnp.concatenate([x] * lax.axis_size(axis), axis=dim)]
    unnamed x25 -> x38, local copies, waits for them, and re-layouts: 21.7 us -> 21.9 us
  transfers between devices with their start and end apart: 6 -> 6, of which waited for: 4 -> 3; matrix products, arithmetic and copies ran while one was open for 57% -> 50% of each run, Pallas kernels for 0% -> 0%
where the time goes in v1:
time: 205 us; the launch traced here: 203 us
  matrix products  80.7 us (39%)
  local copies, waits for them, and re-layouts  54.4 us (27%)
  starting transfers between devices  32.8 us (16%)
  waiting for transfers between devices  29.5 us (14%)
  other arithmetic  5.67 us (3%)
    dot_general x20, matrix products, local(): jnp.einsum('rcp,cpq->rcq', window, masked, preferred_element_type=jnp.flo...  76.3 us
    all_to_all x1, waiting for transfers between devices, tiled_gather(): return lax.all_to_all(copies, axis, dim, dim, tiled=True)  25.5 us
    unnamed x38, local copies, waits for them, and re-layouts  21.9 us
    all_to_all x1, local copies, waits for them, and re-layouts, local(): lax.all_to_all(four_dim, 'vir', split_axis=3, concat_axis=2, tiled=True)  11.9 us
    reshape x2, local copies, waits for them, and re-layouts, local(): four_dim = amplitudes.reshape(outer_occ, NJ, NB_DEV, NA)  11.2 us
    all_to_all x1, starting transfers between devices, local(): lax.all_to_all(lax.all_to_all(cycle_part, 'occ', split_axis=0, concat_axi...  8.93 us
    all_to_all x1, starting transfers between devices, local(): lax.all_to_all(four_dim, 'vir', split_axis=3, concat_axis=2, tiled=True)  8.45 us
    convert_element_type x2, local copies, waits for them, and re-layouts, local(): cycle_flat.astype(jnp.float32) + ladder  5.31 us
  transfers between devices with their start and end apart: 6, of which 3 were waited for; matrix products, arithmetic and copies ran while one was open for 50% of the time, Pallas kernels for 0%

profile of v1, /device:TPU:1, one launch (start us, length us, event | category | flops | bytes accessed | tf_op | source)
XLA Modules:
  0.0 203.4 jit_solution(13714625920768086906)
XLA Ops:
  0.0 0.8 fusion.152
  0.8 4.9 %collective-permute-start = (bf16[64,256]{1,0:T(8,128)(2,1)S(1)}, bf16[64,256]{1,0:T(8,128)(2,1)S(1)}, u32[]{:S(2)}, u32[]{:S(2)}) collective-permute-start(bf16[64,256]{1,0:T(8,128)(2,1)S(1)} %get-tuple-element.11), channel_id=1, source_target_pairs={{0,1},{1,2},{2,3},{3,4},{4,5},{5,6},{6,7},{7,8},{8,9},{9,10},{10,1... | collective-permute-start | bytes 98312 | tf_op jit(solution)/shard_map/ppermute | solution.py:24
  5.7 1.9 collective-permute-start.1
  7.6 1.8 reshape.294
  9.5 9.4 %copy.132 = bf16[4,16,2,4096]{1,0,2,3:T(4,128)(2,1)} copy(bf16[4,16,2,4096]{3,2,1,0:T(2,128)(2,1)S(1)} %reshape.294) | data formatting | bytes 2097152 | tf_op jit(solution)/shard_map/reshape | solution.py:38
  18.9 11.2 %reshape.306 = bf16[32,2,8192]{2,1,0:T(2,128)(2,1)} reshape(bf16[4096,2,4,16]{3,2,1,0:T(4,128)(2,1)} %bitcast.217) | data formatting | bytes 2097152
  30.1 8.4 %all-to-all-start = ((bf16[32,2,8192]{2,1,0:T(2,128)(2,1)}), bf16[32,2,8192]{2,1,0:T(2,128)(2,1)S(1)}, u32[]{:S(2)}, u32[]{:S(2)}) async-start(bf16[32,2,8192]{2,1,0:T(2,128)(2,1)} %reshape.306), calls=%async_computation | async-start | bytes 2097152 | tf_op jit(solution)/shard_map/all_to_all | solution.py:39
  38.6 0.0 copy-done.11
  38.6 0.0 copy-done.9
  38.6 0.0 copy-done
  38.7 3.7 %fusion.12 = f32[64,128,64]{1,2,0:T(8,128)} fusion(pred[64]{0:T(512)(128)(4,1)S(1)} %get-tuple-element.23, bf16[64,4,128,128]{3,2,1,0:T(8,128)(2,1)} %param.9, bf16[64,8192]{1,0:T(8,128)(2,1)S(1)} %copy-done), kind=kOutput, calls=%fused_computation.24 | convolution fusion | flops 135266304 | bytes 5242944 | tf_op jit(solution)/shard_map/rcp,cpq->rcq/dot_general | solution.py:55
  42.4 3.6 %fusion.17 = f32[64,128,64]{1,2,0:T(8,128)} fusion(pred[64]{0:T(512)(128)(4,1)S(1)} %get-tuple-element.15, bf16[64,4,128,128]{3,2,1,0:T(8,128)(2,1)} %param.9, bf16[64,8192]{1,0:T(8,128)(2,1)S(1)} %copy-done), kind=kOutput, calls=%fused_computation.34 | convolution fusion | flops 135266304 | bytes 5242944 | tf_op jit(solution)/shard_map/rcp,cpq->rcq/dot_general | solution.py:55
  46.0 3.7 %fusion.23 = f32[64,128,64]{1,2,0:T(8,128)} fusion(pred[64]{0:T(512)(128)(4,1)S(1)} %get-tuple-element.19, bf16[64,4,128,128]{3,2,1,0:T(8,128)(2,1)} %param.9, bf16[64,8192]{1,0:T(8,128)(2,1)S(1)} %copy-done), kind=kOutput, calls=%fused_computation.49 | convolution fusion | flops 135266304 | bytes 5242944 | tf_op jit(solution)/shard_map/rcp,cpq->rcq/dot_general | solution.py:55
  49.7 3.8 %fusion.7 = f32[64,128,64]{1,2,0:T(8,128)} fusion(pred[64]{0:T(512)(128)(4,1)S(1)} %get-tuple-element.27, bf16[64,4,128,128]{3,2,1,0:T(8,128)(2,1)} %param.9, bf16[64,8192]{1,0:T(8,128)(2,1)S(1)} %copy-done), kind=kOutput, calls=%fused_computation.14 | convolution fusion | flops 135266304 | bytes 5242944 | tf_op jit(solution)/shard_map/rcp,cpq->rcq/dot_general | solution.py:55
  53.5 0.0 copy-done.3
  53.5 1.5 copy.134
  55.0 0.0 collective-permute-done
  55.0 0.1 constant_dynamic-update-slice_fusion
  55.1 0.0 collective-permute-done.1
  55.2 0.0 slice-start
  55.2 0.4 slice_bitcast_fusion.1
  55.5 0.0 copy-start.5
  55.6 0.0 copy-start.1
  55.6 0.0 slice-start.1
  55.6 4.7 %fusion.13 = f32[64,128,64]{1,2,0:T(8,128)} fusion(pred[64]{0:T(512)(128)(4,1)S(1)} %get-tuple-element.24, bf16[64,4,128,128]{3,2,1,0:T(8,128)(2,1)} %param.9, bf16[8,64,8,128]{3,2,1,0:T(8,128)(2,1)S(1)} %get-tuple-element.7), kind=kOutput, calls=%fused_computation.25 | convolution fusion | flops 135266304 | bytes 5242944 | tf_op jit(solution)/shard_map/rcp,cpq->rcq/dot_general | solution.py:55
  60.3 0.0 copy-done.5
  60.3 3.8 %fusion.18 = f32[64,128,64]{1,2,0:T(8,128)} fusion(pred[64]{0:T(512)(128)(4,1)S(1)} %get-tuple-element.16, bf16[64,4,128,128]{3,2,1,0:T(8,128)(2,1)} %param.9, bf16[8,64,8,128]{3,2,1,0:T(8,128)(2,1)S(1)} %get-tuple-element.7), kind=kOutput, calls=%fused_computation.35 | convolution fusion | flops 135266304 | bytes 5242944 | tf_op jit(solution)/shard_map/rcp,cpq->rcq/dot_general | solution.py:55
  64.0 0.0 slice-done
  64.0 2.1 %fusion.14 = f32[64,128,64]{1,2,0:T(8,128)} fusion(pred[64]{0:T(512)(128)(4,1)S(1)} %get-tuple-element.25, bf16[64,4,128,128]{3,2,1,0:T(8,128)(2,1)S(1)} %bitcast.224, bf16[8,64,8,128]{3,2,1,0:T(8,128)(2,1)S(1)} %get-tuple-element.8), kind=kOutput, calls=%fused_computation.26 | convolution fusion | flops 135266304 | bytes 5243392 | tf_op jit(solution)/shard_map/rcp,cpq->rcq/dot_general | solution.py:55
  66.1 2.1 %fusion.19 = f32[64,128,64]{1,2,0:T(8,128)} fusion(pred[64]{0:T(512)(128)(4,1)S(1)} %get-tuple-element.17, bf16[64,4,128,128]{3,2,1,0:T(8,128)(2,1)S(1)} %bitcast.224, bf16[8,64,8,128]{3,2,1,0:T(8,128)(2,1)S(1)} %get-tuple-element.8), kind=kOutput, calls=%fused_computation.36 | convolution fusion | flops 135266304 | bytes 5243392 | tf_op jit(solution)/shard_map/rcp,cpq->rcq/dot_general | solution.py:55
  68.2 0.0 all-to-all-done
  68.2 7.6 %reshape.307 = bf16[4096,2,4,16]{3,2,1,0:T(4,128)(2,1)} reshape(bf16[32,2,8192]{2,1,0:T(2,128)(2,1)S(1)} %all-to-all-done) | data formatting | bytes 2097152
  75.8 11.9 %copy.133 = bf16[4,16,2,32,128]{4,2,3,1,0:T(2,128)(2,1)S(1)} copy(bf16[4,16,2,32,128]{1,0,2,4,3:T(4,128)(2,1)} %bitcast.218) | data formatting | bytes 2097152 | tf_op jit(solution)/shard_map/all_to_all | solution.py:39
  87.8 2.3 %pad_maximum_fusion = bf16[16,16,64,128]{3,2,1,0:T(8,128)(2,1)} fusion(bf16[4,16,64,128]{3,2,1,0:T(8,128)(2,1)S(1)} %bitcast.219), kind=kLoop, calls=%fused_computation | loop fusion | flops 6291456 | bytes 5242880 | tf_op jit(solution)/shard_map/concatenate | solution.py:15
  90.0 5.0 %all-to-all-start.1 = ((bf16[16,16,64,128]{3,2,1,0:T(8,128)(2,1)}), bf16[16,16,64,128]{3,2,1,0:T(8,128)(2,1)}, u32[]{:S(2)}, u32[]{:S(2)}) async-start(bf16[16,16,64,128]{3,2,1,0:T(8,128)(2,1)} %pad_maximum_fusion), calls=%async_computation.1 | async-start | bytes 8388608 | tf_op jit(solution)/shard_map/all_to_all | solution.py:16
  95.1 0.3 slice_bitcast_fusion.3
  95.4 0.0 copy-start.7
  95.4 0.9 copy-done.6
  96.3 3.8 %fusion.24 = f32[64,128,64]{1,2,0:T(8,128)} fusion(pred[64]{0:T(512)(128)(4,1)S(1)} %get-tuple-element.20, bf16[64,4,128,128]{3,2,1,0:T(8,128)(2,1)} %param.9, bf16[8,64,8,128]{3,2,1,0:T(8,128)(2,1)S(1)} %copy-done.6), kind=kOutput, calls=%fused_computation.50 | convolution fusion | flops 135266304 | bytes 5242944 | tf_op jit(solution)/shard_map/rcp,cpq->rcq/dot_general | solution.py:55
  100.1 3.9 %fusion.8 = f32[64,128,64]{1,2,0:T(8,128)} fusion(pred[64]{0:T(512)(128)(4,1)S(1)} %get-tuple-element.28, bf16[64,4,128,128]{3,2,1,0:T(8,128)(2,1)} %param.9, bf16[8,64,8,128]{3,2,1,0:T(8,128)(2,1)S(1)} %copy-done.6), kind=kOutput, calls=%fused_computation.15 | convolution fusion | flops 135266304 | bytes 5242944 | tf_op jit(solution)/shard_map/rcp,cpq->rcq/dot_general | solution.py:55
  104.0 3.7 %fusion.9 = f32[64,128,64]{1,2,0:T(8,128)} fusion(pred[64]{0:T(512)(128)(4,1)S(1)} %get-tuple-element.29, bf16[64,4,128,128]{3,2,1,0:T(8,128)(2,1)} %param.9, bf16[8,64,8,128]{3,2,1,0:T(8,128)(2,1)S(1)} %copy-done.2), kind=kOutput, calls=%fused_computation.16 | convolution fusion | flops 135266304 | bytes 5242944 | tf_op jit(solution)/shard_map/rcp,cpq->rcq/dot_general | solution.py:55
  107.7 2.1 %fusion.11 = f32[64,128,64]{1,2,0:T(8,128)} fusion(pred[64]{0:T(512)(128)(4,1)S(1)} %get-tuple-element.21, bf16[64,4,128,128]{3,2,1,0:T(8,128)(2,1)S(1)} %bitcast.226, bf16[8,64,8,128]{3,2,1,0:T(8,128)(2,1)S(1)} %get-tuple-element.6), kind=kOutput, calls=%fused_computation.23 | convolution fusion | flops 135266304 | bytes 5243392 | tf_op jit(solution)/shard_map/rcp,cpq->rcq/dot_general | solution.py:55
  109.8 2.1 %fusion.16 = f32[64,128,64]{1,2,0:T(8,128)} fusion(pred[64]{0:T(512)(128)(4,1)S(1)} %get-tuple-element.14, bf16[64,4,128,128]{3,2,1,0:T(8,128)(2,1)S(1)} %bitcast.226, bf16[8,64,8,128]{3,2,1,0:T(8,128)(2,1)S(1)} %get-tuple-element.6), kind=kOutput, calls=%fused_computation.33 | convolution fusion | flops 135266304 | bytes 5243392 | tf_op jit(solution)/shard_map/rcp,cpq->rcq/dot_general | solution.py:55
  111.9 2.1 %fusion.22 = f32[64,128,64]{1,2,0:T(8,128)} fusion(pred[64]{0:T(512)(128)(4,1)S(1)} %get-tuple-element.18, bf16[64,4,128,128]{3,2,1,0:T(8,128)(2,1)S(1)} %bitcast.226, bf16[8,64,8,128]{3,2,1,0:T(8,128)(2,1)S(1)} %get-tuple-element.6), kind=kOutput, calls=%fused_computation.48 | convolution fusion | flops 135266304 | bytes 5243392 | tf_op jit(solution)/shard_map/rcp,cpq->rcq/dot_general | solution.py:55
  113.9 2.1 %fusion.21 = f32[64,128,64]{1,2,0:T(8,128)} fusion(pred[64]{0:T(512)(128)(4,1)S(1)} %get-tuple-element.22, bf16[64,4,128,128]{3,2,1,0:T(8,128)(2,1)S(1)} %bitcast.226, bf16[8,64,8,128]{3,2,1,0:T(8,128)(2,1)S(1)} %get-tuple-element.5), kind=kOutput, calls=%fused_computation.47 | convolution fusion | flops 135266304 | bytes 5243392 | tf_op jit(solution)/shard_map/rcp,cpq->rcq/dot_general | solution.py:55
  116.1 2.0 %fusion.5 = f32[64,128,64]{1,2,0:T(8,128)} fusion(pred[64]{0:T(512)(128)(4,1)S(1)} %get-tuple-element.30, bf16[64,4,128,128]{3,2,1,0:T(8,128)(2,1)S(1)} %bitcast.226, bf16[8,64,8,128]{3,2,1,0:T(8,128)(2,1)S(1)} %get-tuple-element.5), kind=kOutput, calls=%fused_computation.12 | convolution fusion | flops 135266304 | bytes 5243392 | tf_op jit(solution)/shard_map/rcp,cpq->rcq/dot_general | solution.py:55
  118.1 25.5 %all-to-all-done.1 = bf16[16,16,64,128]{3,2,1,0:T(8,128)(2,1)} async-done(((bf16[16,16,64,128]{3,2,1,0:T(8,128)(2,1)}), bf16[16,16,64,128]{3,2,1,0:T(8,128)(2,1)}, u32[]{:S(2)}, u32[]{:S(2)}) %all-to-all-start.1) | async-done | bytes 4194336 | tf_op jit(solution)/shard_map/all_to_all | solution.py:16
  143.7 0.0 copy-done.4
  143.7 4.5 %fusion.48 = bf16[16,4,64,128]{3,2,1,0:T(8,128)(2,1)} fusion(bf16[16,16,64,128]{3,2,1,0:T(8,128)(2,1)} %all-to-all-done.1, bf16[16,64,4,64]{1,3,0,2:T(8,128)(2,1)S(1)} %copy-done.4), kind=kOutput, calls=%fused_computation.73 | convolution fusion | flops 1074266112 | bytes 5767168 | tf_op jit(solution)/shard_map/ijba,jbkc->ikca/dot_general | solution.py:60
  148.1 3.5 %all-to-all-start.2 = ((bf16[16,4,64,128]{3,2,1,0:T(8,128)(2,1)}), bf16[16,4,64,128]{3,2,1,0:T(8,128)(2,1)S(1)}, u32[]{:S(2)}, u32[]{:S(2)}) async-start(bf16[16,4,64,128]{3,2,1,0:T(8,128)(2,1)} %fusion.48), calls=%async_computation.2 | async-start | bytes 2097152 | tf_op jit(solution)/shard_map/all_to_all | solution.py:64
  151.6 4.0 %fusion.6 = f32[64,128,64]{1,2,0:T(8,128)} fusion(pred[64]{0:T(512)(128)(4,1)S(1)} %get-tuple-element.26, bf16[64,4,128,128]{3,2,1,0:T(8,128)(2,1)} %param.9, bf16[8,64,8,128]{3,2,1,0:T(8,128)(2,1)} %copy-done.7), kind=kOutput, calls=%fused_computation.13 | convolution fusion | flops 135266304 | bytes 5242944 | tf_op jit(solution)/shard_map/rcp,cpq->rcq/dot_general | solution.py:55
  155.7 3.7 %fusion.10 = f32[64,128,64]{1,2,0:T(8,128)} fusion(pred[64]{0:T(512)(128)(4,1)S(1)} %get-tuple-element.32, bf16[64,4,128,128]{3,2,1,0:T(8,128)(2,1)} %param.9, bf16[8,64,8,128]{3,2,1,0:T(8,128)(2,1)S(1)} %get-tuple-element.5), kind=kOutput, calls=%fused_computation.22 | convolution fusion | flops 135266304 | bytes 5242944 | tf_op jit(solution)/shard_map/rcp,cpq->rcq/dot_general | solution.py:55
  159.3 3.7 %fusion.15 = f32[64,128,64]{1,2,0:T(8,128)} fusion(pred[64]{0:T(512)(128)(4,1)S(1)} %get-tuple-element.31, bf16[64,4,128,128]{3,2,1,0:T(8,128)(2,1)} %param.9, bf16[8,64,8,128]{3,2,1,0:T(8,128)(2,1)S(1)} %get-tuple-element.5), kind=kOutput, calls=%fused_computation.32 | convolution fusion | flops 135266304 | bytes 5242944 | tf_op jit(solution)/shard_map/rcp,cpq->rcq/dot_general | solution.py:55
  163.1 2.6 %all-to-all-done.2 = bf16[16,4,64,128]{3,2,1,0:T(8,128)(2,1)S(1)} async-done(((bf16[16,4,64,128]{3,2,1,0:T(8,128)(2,1)}), bf16[16,4,64,128]{3,2,1,0:T(8,128)(2,1)S(1)}, u32[]{:S(2)}, u32[]{:S(2)}) %all-to-all-start.2) | async-done | bytes 1048608 | tf_op jit(solution)/shard_map/all_to_all | solution.py:64
  165.7 0.1 copy.135
  165.8 1.6 copy.136
  167.4 8.9 %all-to-all-start.3 = ((bf16[4,16,64,128]{3,1,0,2:T(8,128)(2,1)}), bf16[4,16,64,128]{3,1,0,2:T(8,128)(2,1)}, u32[]{:S(2)}, u32[]{:S(2)}) async-start(bf16[4,16,64,128]{3,1,0,2:T(8,128)(2,1)} %copy.136), calls=%async_computation.3 | async-start | bytes 2097152 | tf_op jit(solution)/shard_map/all_to_all | solution.py:63
  176.4 15.6 %fusion.20 = f32[64,8,8,128]{3,2,1,0:T(8,128)S(1)} fusion(f32[64,128,64]{1,2,0:T(8,128)} %fusion.9, f32[64,128,64]{1,2,0:T(8,128)} %fusion.14, f32[64,128,64]{1,2,0:T(8,128)} %fusion.19, f32[64,128,64]{1,2,0:T(8,128)} %fusion.8, f32[64,128,64]{1,2,0:T(8,128)} %fusion.13, f32[64,128,64]{1,2,0:T(8,128)} %fusion.24, f32[64,128,64]{1,2,0:T(8,128)} %fusion.18, ...), kind=kOutput, calls=%fused_computation.39 | convolution fusion | flops 145227776 | bytes 45088832 | tf_op jit(solution)/shard_map/rcp,cpq->rcq/dot_general | solution.py:55
  192.0 1.3 all-to-all-done.3
  193.3 1.4 copy.137
  194.7 0.3 convert_bitcast_fusion
  195.0 2.6 %copy.138 = f32[4,16,2,32,128]{4,3,2,1,0:T(8,128)} copy(f32[4,16,2,32,128]{4,1,2,3,0:T(8,128)S(1)} %convert_bitcast_fusion) | data formatting | bytes 4194304 | tf_op jit(solution)/shard_map/convert_element_type | solution.py:73
  197.6 2.7 %reshape.301 = f32[64,8192]{1,0:T(8,128)} reshape(f32[4,16,2,32,128]{4,3,2,1,0:T(8,128)} %copy.138) | data formatting | bytes 4194304 | tf_op jit(solution)/shard_map/convert_element_type | solution.py:73
  200.3 3.1 %fusion.4 = bf16[64,8192]{1,0:T(8,128)(2,1)} fusion(f32[64,8192]{1,0:T(8,128)} %reshape.301, f32[64,8,8,128]{3,2,1,0:T(8,128)S(1)} %fusion.20, bf16[64,8192]{1,0:T(8,128)(2,1)S(1)} %copy-done, f32[8192]{0:T(1024)S(1)} %copy-done.8, f32[64]{0:T(128)S(1)} %copy-done.10), kind=kLoop, calls=%fused_computation.6 | loop fusion | flops 3145728 | bytes 6324480 | tf_op jit(solution)/shard_map/convert_element_type | solution.py:75
  (29 shorter events, 0.1 us)
Async XLA Ops:
  0.8 54.2 %collective-permute-start = (bf16[64,256]{1,0:T(8,128)(2,1)S(1)}, bf16[64,256]{1,0:T(8,128)(2,1)S(1)}, u32[]{:S(2)}, u32[]{:S(2)}) collective-permute-start(bf16[64,256]{1,0:T(8,128)(2,1)S(1)} %get-tuple-element.11), channel_id=1, source_target_pairs={{0,1},{1,2},{2,3},{3,4},{4,5},{5,6},{6,7},{7,8},{8,9},{9,10},{10,1... | collective-permute-start | bytes 98312 | tf_op jit(solution)/shard_map/ppermute | solution.py:24
  5.7 49.4 %collective-permute-start.1 = (bf16[64,256]{1,0:T(8,128)(2,1)S(1)}, bf16[64,256]{1,0:T(8,128)(2,1)S(1)}, u32[]{:S(2)}, u32[]{:S(2)}) collective-permute-start(bf16[64,256]{1,0:T(8,128)(2,1)S(1)} %get-tuple-element.12), channel_id=1, source_target_pairs={{1,0},{2,1},{3,2},{4,3},{5,4},{6,5},{7,6},{8,7},{9,8},{10,9},{11,1... | collective-permute-start | bytes 98312 | tf_op jit(solution)/shard_map/ppermute | solution.py:27
  30.1 8.5 %copy-start.11 = (s32[64]{0:T(128)S(1)}, s32[64]{0:T(128)}, u32[]{:S(2)}) copy-start(s32[64]{0:T(128)} %param.11) | copy-start | bytes 772
  30.1 8.5 %copy-start.9 = (s32[64,4]{0,1:T(4,128)S(1)}, s32[64,4]{0,1:T(4,128)}, u32[]{:S(2)}) copy-start(s32[64,4]{0,1:T(4,128)} %param.10) | copy-start | bytes 3076
  30.1 8.6 %copy-start = (bf16[64,8192]{1,0:T(8,128)(2,1)S(1)}, bf16[64,8192]{1,0:T(8,128)(2,1)}, u32[]{:S(2)}) copy-start(bf16[64,8192]{1,0:T(8,128)(2,1)} %param.7) | copy-start | bytes 3145732
  30.1 38.1 %all-to-all-start = ((bf16[32,2,8192]{2,1,0:T(2,128)(2,1)}), bf16[32,2,8192]{2,1,0:T(2,128)(2,1)S(1)}, u32[]{:S(2)}, u32[]{:S(2)}) async-start(bf16[32,2,8192]{2,1,0:T(2,128)(2,1)} %reshape.306), calls=%async_computation | async-start | bytes 2097152 | tf_op jit(solution)/shard_map/all_to_all | solution.py:39
  49.7 3.8 %copy-start.3 = (bf16[16,64,4,64]{3,2,1,0:T(4,128)(2,1)S(1)}, bf16[16,64,4,64]{3,2,1,0:T(4,128)(2,1)}, u32[]{:S(2)}) copy-start(bf16[16,64,4,64]{3,2,1,0:T(4,128)(2,1)} %param.8) | copy-start | bytes 1572868
  55.2 8.9 %slice-start = ((s8[8388608]{0:T(1024)(128)(4,1)}), s8[4194304]{0:T(1024)(128)(4,1)S(1)}, s32[]{:S(2)}) async-start(s8[8388608]{0:T(1024)(128)(4,1)} %bitcast.223), calls=%async_computation.4 | async-start | bytes 8388608
  55.5 4.7 %copy-start.5 = (bf16[8,64,8,128]{3,2,1,0:T(8,128)(2,1)}, bf16[8,64,8,128]{3,2,1,0:T(8,128)(2,1)S(1)}, u32[]{:S(2)}) copy-start(bf16[8,64,8,128]{3,2,1,0:T(8,128)(2,1)S(1)} %get-tuple-element.7) | copy-start | bytes 3145732
  55.6 10.6 %copy-start.1 = (bf16[8,64,8,128]{3,2,1,0:T(8,128)(2,1)}, bf16[8,64,8,128]{3,2,1,0:T(8,128)(2,1)S(1)}, u32[]{:S(2)}) copy-start(bf16[8,64,8,128]{3,2,1,0:T(8,128)(2,1)S(1)} %get-tuple-element.8) | copy-start | bytes 3145732
  55.6 8.5 %slice-start.1 = ((s8[8388608]{0:T(1024)(128)(4,1)}), s8[4194304]{0:T(1024)(128)(4,1)S(1)}, s32[]{:S(2)}) async-start(s8[8388608]{0:T(1024)(128)(4,1)} %bitcast.223), calls=%async_computation.5 | async-start | bytes 8388608
  90.0 53.6 %all-to-all-start.1 = ((bf16[16,16,64,128]{3,2,1,0:T(8,128)(2,1)}), bf16[16,16,64,128]{3,2,1,0:T(8,128)(2,1)}, u32[]{:S(2)}, u32[]{:S(2)}) async-start(bf16[16,16,64,128]{3,2,1,0:T(8,128)(2,1)} %pad_maximum_fusion), calls=%async_computation.1 | async-start | bytes 8388608 | tf_op jit(solution)/shard_map/all_to_all | solution.py:16
  95.1 1.2 copy-start.6
  95.4 16.5 %copy-start.7 = (bf16[8,64,8,128]{3,2,1,0:T(8,128)(2,1)}, bf16[8,64,8,128]{3,2,1,0:T(8,128)(2,1)S(1)}, u32[]{:S(2)}) copy-start(bf16[8,64,8,128]{3,2,1,0:T(8,128)(2,1)S(1)} %get-tuple-element.6) | copy-start | bytes 3145732
  96.3 11.4 %slice-start.2 = ((s8[8388608]{0:T(1024)(128)(4,1)}), s8[4194304]{0:T(1024)(128)(4,1)S(1)}, s32[]{:S(2)}) async-start(s8[8388608]{0:T(1024)(128)(4,1)} %bitcast.225), calls=%async_computation.6 | async-start | bytes 8388608
  100.1 3.9 %copy-start.2 = (bf16[8,64,8,128]{3,2,1,0:T(8,128)(2,1)S(1)}, bf16[8,64,8,128]{3,2,1,0:T(8,128)(2,1)}, u32[]{:S(2)}) copy-start(bf16[8,64,8,128]{3,2,1,0:T(8,128)(2,1)} %copy-done.1) | copy-start | bytes 3145732
  100.1 7.6 %slice-start.3 = ((s8[8388608]{0:T(1024)(128)(4,1)}), s8[4194304]{0:T(1024)(128)(4,1)S(1)}, s32[]{:S(2)}) async-start(s8[8388608]{0:T(1024)(128)(4,1)} %bitcast.225), calls=%async_computation.7 | async-start | bytes 8388608
  116.1 27.6 %copy-start.4 = (bf16[16,64,4,64]{1,3,0,2:T(8,128)(2,1)S(1)}, bf16[16,64,4,64]{1,3,0,2:T(8,128)(2,1)}, u32[]{:S(2)}) copy-start(bf16[16,64,4,64]{1,3,0,2:T(8,128)(2,1)} %copy.134) | copy-start | bytes 1572868
  148.1 17.6 %all-to-all-start.2 = ((bf16[16,4,64,128]{3,2,1,0:T(8,128)(2,1)}), bf16[16,4,64,128]{3,2,1,0:T(8,128)(2,1)S(1)}, u32[]{:S(2)}, u32[]{:S(2)}) async-start(bf16[16,4,64,128]{3,2,1,0:T(8,128)(2,1)} %fusion.48), calls=%async_computation.2 | async-start | bytes 2097152 | tf_op jit(solution)/shard_map/all_to_all | solution.py:64
  167.4 25.9 %all-to-all-start.3 = ((bf16[4,16,64,128]{3,1,0,2:T(8,128)(2,1)}), bf16[4,16,64,128]{3,1,0,2:T(8,128)(2,1)}, u32[]{:S(2)}, u32[]{:S(2)}) async-start(bf16[4,16,64,128]{3,1,0,2:T(8,128)(2,1)} %copy.136), calls=%async_computation.3 | async-start | bytes 2097152 | tf_op jit(solution)/shard_map/all_to_all | solution.py:63
  197.6 2.8 %copy-start.8 = (f32[8192]{0:T(1024)S(1)}, f32[8192]{0:T(1024)}, u32[]{:S(2)}) copy-start(f32[8192]{0:T(1024)} %param.13) | copy-start | bytes 98308
  197.6 2.8 %copy-start.10 = (f32[64]{0:T(128)S(1)}, f32[64]{0:T(128)}, u32[]{:S(2)}) copy-start(f32[64]{0:T(128)} %param.12) | copy-start | bytes 772
